TPU v7x, 32 devices: a whole 2x2x4 slice. The times are simulated.
32 devices in a mesh: tok: 4 (over y, x), col: 8 (over z, core).
Axes of the slice: x: 2, y: 2, z: 4, core: 2. Of those that a mesh axis runs over, the one named last changes fastest.
Arguments:
- activations: bfloat16 [8192, 8192], P('tok', 'col'), may hold values from -60 to 60, as said below
- weight: bfloat16 [8192, 8192], P('tok', 'col'), may hold values from -6 to 6
- keep_mask: int32 [8192, 8192], P('tok', 'col'), may hold values from 0 to 1
Outputs:
- new_weight: bfloat16 [8192, 8192], P('tok', 'col')
Inputs may be any that keep to these rules, and one draw needn't show every extreme that they name: activations of calibration tokens.
All inputs are finite; a program needn't handle non-finite values.
Results may differ from a plain program's by a relative error of at most 0.00115.
Values may be sent and summed in bfloat16 or wider, within the bound.
No kernel may reach another device: no remote copies, remote signals or barrier semaphores. Data moves between devices by JAX's collectives and lax.ppermute only.
A program may use at most 128 MiB of HBM per device.

v0:
```python
import jax
import jax.numpy as jnp
from jax import lax
from jax.sharding import PartitionSpec as P

B = 1024
ITERS = 4


def per_device(activations, weight, keep_mask):
    highest = lax.Precision.HIGHEST
    n_col = lax.axis_size("col")
    n_tok = lax.axis_size("tok")
    tok_rows = activations.shape[0]
    panel_width = B // n_col
    total_count = tok_rows * n_tok
    partial_panel = lax.dot_general(
        activations,
        lax.all_gather(activations[:, :panel_width], "col", axis=1, tiled=True),
        (((0,), (0,)), ((), ())),
        preferred_element_type=jnp.float32,
    )
    block_part = lax.psum(partial_panel[:panel_width], "tok") / total_count
    diagonal_block = lax.all_gather(block_part, "col", axis=0, tiled=True)
    identity = jnp.eye(B, dtype=jnp.float32)
    damping = 0.01 * jnp.mean(jnp.diagonal(diagonal_block))
    damped = diagonal_block + damping * identity
    frobenius = jnp.sqrt(jnp.sum(damped * damped))
    col_index = lax.axis_index("col")
    row_ids = col_index * panel_width + lax.iota(jnp.int32, panel_width)
    iterate = (row_ids[:, None] == lax.iota(jnp.int32, B)[None, :]).astype(jnp.float32) / frobenius
    for sweep in range(ITERS):
        if sweep == 0:
            whole = identity / frobenius
        else:
            whole = lax.all_gather(iterate.astype(jnp.bfloat16), "col", axis=0, tiled=True).astype(
                iterate.dtype
            )
        product = jnp.dot(iterate, damped, precision=highest)
        iterate = 2.0 * iterate - jnp.dot(product, whole, precision=highest)
    inverse = lax.all_gather(iterate, "col", axis=0, tiled=True)
    remainder = lax.psum(partial_panel[panel_width:], "tok") / total_count
    hessian_panel = jnp.concatenate([block_part, remainder], axis=0)
    pruned = jnp.where(
        keep_mask[:, :panel_width] == 0, weight[:, :panel_width], jnp.zeros((), jnp.bfloat16)
    )
    pruned_panel = lax.all_gather(pruned, "col", axis=1, tiled=True).astype(jnp.float32)
    factor_rows = jnp.dot(pruned_panel, inverse, precision=highest)
    correction = lax.dot_general(
        factor_rows, hessian_panel, (((1,), (1,)), ((), ())), precision=highest
    )
    kept = keep_mask.astype(jnp.float32)
    return (kept * (weight.astype(jnp.float32) - correction)).astype(jnp.bfloat16)


def solution(mesh):
    return jax.shard_map(
        per_device,
        mesh=mesh,
        in_specs=(P("tok", "col"), P("tok", "col"), P("tok", "col")),
        out_specs=P("tok", "col"),
        check_vma=False,
    )
```

profile of v0, /device:TPU:0, one launch (start us, length us, event | category | flops | bytes accessed | tf_op | source)
XLA Modules:
  0.0 493.3 jit_solution(1033233946870937970)
XLA Ops:
  6.5 0.0 all-gather.10.cloned.1.call-start
  6.5 1.9 slice.17
  8.4 0.0 all-gather.10.cloned.1.call-update
  8.4 0.0 all-reduce.3.cloned.1.call-start
  8.5 51.0 %all-gather.10.cloned.1.call-done = bf16[2048,1024]{1,0:T(8,128)(2,1)} async-done(((bf16[2048,128]{1,0:T(8,128)(2,1)}), bf16[2048,1024]{1,0:T(8,128)(2,1)}) %all-gather.10.cloned.1.call-update) | async-done | bytes 4194320 | tf_op jit(solution)/shard_map/all_gather | solution.py:19
  59.5 7.6 %fusion.31 = f32[1024,1024]{1,0:T(8,128)S(1)} fusion(bf16[2048,1024]{1,0:T(8,128)(2,1)} %param.3, bf16[2048,1024]{1,0:T(8,128)(2,1)} %all-gather.10.cloned.1.call-done), kind=kOutput, calls=%fused_computation.42 | convolution fusion | flops 4294967296 | bytes 12582912 | tf_op jit(solution)/shard_map/dot_general | solution.py:17
  67.1 0.8 slice.22
  67.9 2.3 slice.23
  70.2 0.0 all-reduce.3.cloned.1.call-update
  70.2 0.0 all-gather.12.cloned.1.call-start
  70.3 101.9 %all-reduce.3.cloned.1.call-done = (f32[128,1024]{1,0:T(8,128)}, f32[896,1024]{1,0:T(8,128)}) async-done(((f32[128,1024]{1,0:T(8,128)}, f32[896,1024]{1,0:T(8,128)}), (f32[128,1024]{1,0:T(8,128)}, f32[896,1024]{1,0:T(8,128)})) %all-reduce.3.cloned.1.call-update) | async-done | bytes 4194320 | tf_op jit(solution)/shard_map/psum | solution.py:23
  172.2 1.9 broadcast_multiply_fusion.1
  174.1 0.0 all-gather.12.cloned.1.call-update
  174.1 0.0 all-gather.14.cloned.1.call-start
  174.2 46.9 %all-gather.12.cloned.1.call-done = f32[1024,1024]{1,0:T(8,128)} async-done(((f32[128,1024]{1,0:T(8,128)}), f32[1024,1024]{1,0:T(8,128)}) %all-gather.12.cloned.1.call-update) | async-done | bytes 4194320 | tf_op jit(solution)/shard_map/all_gather | solution.py:24
  221.2 17.1 %gather_fusion = f32[1024]{0:T(1024)S(1)} fusion(f32[1024,1024]{1,0:T(8,128)} %all-gather.12.cloned.1.call-done, s32[1024]{0:T(1024)S(1)} %bitcast.16), kind=kCustom, calls=%fused_computation | custom fusion | bytes 16384 | tf_op jit(solution)/shard_map/jit(diagonal)/cond/branch_0_fun/gather | solution.py:26
  238.2 0.6 reduce_sum.18
  239.5 3.9 multiply_reduce_fusion
  244.0 4.7 fusion.16
  248.8 2.5 fusion.28
  251.3 0.0 all-gather.14.cloned.1.call-update
  251.3 0.0 all-gather.16.cloned.1.call-start
  251.3 4.7 fusion.15
  256.0 23.4 %all-gather.14.cloned.1.call-done = bf16[1024,1024]{1,0:T(8,128)(2,1)} async-done(((bf16[128,1024]{1,0:T(8,128)(2,1)}), bf16[1024,1024]{1,0:T(8,128)(2,1)}) %all-gather.14.cloned.1.call-update) | async-done | bytes 2097168 | tf_op jit(solution)/shard_map/all_gather | solution.py:36
  279.4 3.3 fusion.29
  282.7 0.0 all-gather.16.cloned.1.call-update
  282.8 0.2 all-gather.18.cloned.1.call-start
  283.0 4.7 fusion.14
  287.7 23.8 %all-gather.16.cloned.1.call-done = bf16[1024,1024]{1,0:T(8,128)(2,1)} async-done(((bf16[128,1024]{1,0:T(8,128)(2,1)}), bf16[1024,1024]{1,0:T(8,128)(2,1)}) %all-gather.16.cloned.1.call-update) | async-done | bytes 2097168 | tf_op jit(solution)/shard_map/all_gather | solution.py:36
  311.5 3.3 fusion.30
  314.9 0.0 all-gather.18.cloned.1.call-update
  314.9 0.0 all-gather.8.cloned.1.call-start
  314.9 2.3 fusion.17
  317.2 0.0 all-gather.8.cloned.1.call-update
  317.2 0.0 all-gather.20.cloned.1.call-start
  317.3 4.7 fusion.13
  322.0 21.6 %all-gather.18.cloned.1.call-done = bf16[1024,1024]{1,0:T(8,128)(2,1)} async-done(((bf16[128,1024]{1,0:T(8,128)(2,1)}), bf16[1024,1024]{1,0:T(8,128)(2,1)}) %all-gather.18.cloned.1.call-update) | async-done | bytes 2097168 | tf_op jit(solution)/shard_map/all_gather | solution.py:36
  343.6 3.4 convolution_subtract_fusion
  347.0 0.0 all-gather.20.cloned.1.call-update
  347.0 4.6 broadcast_multiply_fusion
  351.6 0.0 copy-start.1
  351.6 40.8 %all-gather.8.cloned.1.call-done = bf16[2048,1024]{1,0:T(8,128)(2,1)} async-done(((bf16[2048,128]{1,0:T(8,128)(2,1)}), bf16[2048,1024]{1,0:T(8,128)(2,1)}) %all-gather.8.cloned.1.call-update) | async-done | bytes 4194320 | tf_op jit(solution)/shard_map/all_gather | solution.py:47
  392.4 46.7 %all-gather.20.cloned.1.call-done = f32[1024,1024]{1,0:T(8,128)} async-done(((f32[128,1024]{1,0:T(8,128)}), f32[1024,1024]{1,0:T(8,128)}) %all-gather.20.cloned.1.call-update) | async-done | bytes 4194320 | tf_op jit(solution)/shard_map/all_gather | solution.py:41
  439.1 0.0 copy-start
  439.1 0.0 copy-start.2
  439.1 16.8 %fusion.32 = f32[2048,1024]{1,0:T(8,128)S(1)} fusion(bf16[2048,1024]{1,0:T(8,128)(2,1)} %all-gather.8.cloned.1.call-done, f32[1024,1024]{1,0:T(8,128)} %all-gather.20.cloned.1.call-done), kind=kOutput, calls=%fused_computation.43 | convolution fusion | flops 25769803776 | bytes 16777216 | tf_op jit(solution)/shard_map/dot_general | solution.py:48
  455.9 0.0 copy-done.1
  455.9 0.0 copy-done
  455.9 0.0 copy-done.2
  455.9 30.5 %multiply_convert_fusion = bf16[2048,1024]{1,0:T(8,128)(2,1)} fusion(bf16[2048,1024]{1,0:T(8,128)(2,1)S(1)} %copy-done.2, s32[2048,1024]{1,0:T(8,128)} %param.5, f32[2048,1024]{1,0:T(8,128)S(1)} %fusion.32, f32[896,1024]{1,0:T(8,128)S(1)} %copy-done, f32[128,1024]{1,0:T(8,128)S(1)} %copy-done.1), kind=kOutput, calls=%fused_computation.1 | convolution fusion | flops 25781338112 | bytes 29360128 | tf_op jit(solution)/shard_map/dot_general | solution.py:49
  (2 shorter events, 0.0 us)
Async XLA Ops:
  6.5 53.0 %all-gather.10.cloned.1.call-start = ((), (), s32[]{:S(2)}) async-start(), calls=%async_computation.1 | async-start | bytes 4718592 | tf_op jit(solution)/shard_map/all_gather | solution.py:19
  8.4 163.8 %all-reduce.3.cloned.1.call-start = ((), (), s32[]{:S(2)}) async-start(), calls=%async_computation.7 | async-start | bytes 8388608 | tf_op jit(solution)/shard_map/psum | solution.py:23
  70.2 150.9 %all-gather.12.cloned.1.call-start = ((), (), s32[]{:S(2)}) async-start(), calls=%async_computation.2 | async-start | bytes 4718592 | tf_op jit(solution)/shard_map/all_gather | solution.py:24
  174.1 105.3 %all-gather.14.cloned.1.call-start = ((), (), s32[]{:S(2)}) async-start(), calls=%async_computation.3 | async-start | bytes 2359296 | tf_op jit(solution)/shard_map/all_gather | solution.py:36
  251.3 60.2 %all-gather.16.cloned.1.call-start = ((), (), s32[]{:S(2)}) async-start(), calls=%async_computation.4 | async-start | bytes 2359296 | tf_op jit(solution)/shard_map/all_gather | solution.py:36
  282.8 60.8 %all-gather.18.cloned.1.call-start = ((), (), s32[]{:S(2)}) async-start(), calls=%async_computation.5 | async-start | bytes 2359296 | tf_op jit(solution)/shard_map/all_gather | solution.py:36
  314.9 77.5 %all-gather.8.cloned.1.call-start = ((), (), s32[]{:S(2)}) async-start(), calls=%async_computation | async-start | bytes 4718592 | tf_op jit(solution)/shard_map/all_gather | solution.py:47
  317.2 121.8 %all-gather.20.cloned.1.call-start = ((), (), s32[]{:S(2)}) async-start(), calls=%async_computation.6 | async-start | bytes 4718592 | tf_op jit(solution)/shard_map/all_gather | solution.py:41
  351.6 104.3 %copy-start.1 = (f32[128,1024]{1,0:T(8,128)S(1)}, f32[128,1024]{1,0:T(8,128)}, u32[]{:S(2)}) copy-start(f32[128,1024]{1,0:T(8,128)} %broadcast_multiply_fusion.1) | copy-start | bytes 1572868
  439.1 16.8 %copy-start = (f32[896,1024]{1,0:T(8,128)S(1)}, f32[896,1024]{1,0:T(8,128)}, u32[]{:S(2)}) copy-start(f32[896,1024]{1,0:T(8,128)} %broadcast_multiply_fusion) | copy-start | bytes 11010052
  439.1 16.8 %copy-start.2 = (bf16[2048,1024]{1,0:T(8,128)(2,1)S(1)}, bf16[2048,1024]{1,0:T(8,128)(2,1)}, u32[]{:S(2)}) copy-start(bf16[2048,1024]{1,0:T(8,128)(2,1)} %param.4) | copy-start | bytes 12582916
Sparse Core Ops, SparseCore 0:
  8.9 50.5 all-gather.9
  70.3 101.8 all-reduce.2
  174.3 46.8 all-gather.11
  251.4 27.9 all-gather.13
  282.9 28.6 all-gather.15
  315.0 28.5 all-gather.17
  345.2 47.2 all-gather.7
  394.0 45.0 all-gather.19
where the time goes:
time: 494 us; the launch traced here: 493 us
  waiting for transfers between devices  356 us (72%)
  matrix products  86.3 us (17%)
  local copies, waits for them, and re-layouts  22.1 us (4%)
  between operations  14.9 us (3%)
  other arithmetic  13.3 us (3%)
    psum x1, waiting for transfers between devices, per_device(): block_part = lax.psum(partial_panel[:panel_width], 'tok') / total_count  102 us
    all_gather x3, waiting for transfers between devices, per_device(): lax.all_gather(iterate.astype(jnp.bfloat16), 'col', axis=0, tiled=True)  68.8 us
    all_gather x1, waiting for transfers between devices, per_device(): lax.all_gather(activations[:, :panel_width], 'col', axis=1, tiled=True)  51 us
    all_gather x1, waiting for transfers between devices, per_device(): diagonal_block = lax.all_gather(block_part, 'col', axis=0, tiled=True)  46.9 us
    all_gather x1, waiting for transfers between devices, per_device(): inverse = lax.all_gather(iterate, 'col', axis=0, tiled=True)  46.7 us
    all_gather x1, waiting for transfers between devices, per_device(): lax.all_gather(pruned, 'col', axis=1, tiled=True).astype(jnp.float32)  40.8 us
    dot_general x1, matrix products, per_device(): lax.dot_general(factor_rows, hessian_panel, (((1,), (1,)), ((), ())), pre...  30.5 us
    dot_general x4, matrix products, per_device(): product = jnp.dot(iterate, damped, precision=highest)  18.8 us
  transfers between devices with their start and end apart: 8, of which 8 were waited for; matrix products, arithmetic and copies ran while one was open for 5% of the time, Pallas kernels for 0%

commit v1 on v0

--- a/solution.py
+++ b/solution.py
@@ -20,7 +20,7 @@
         (((0,), (0,)), ((), ())),
         preferred_element_type=jnp.float32,
     )
-    block_part = lax.psum(partial_panel[:panel_width], "tok") / total_count
+    block_part = jnp.sum(lax.all_gather(partial_panel[:panel_width], "tok"), axis=0) / total_count
     diagonal_block = lax.all_gather(block_part, "col", axis=0, tiled=True)
     identity = jnp.eye(B, dtype=jnp.float32)
     damping = 0.01 * jnp.mean(jnp.diagonal(diagonal_block))

time: 494 us -> 525 us (1.063)
  waiting for transfers between devices: 356 us -> 382 us
    all_gather x0 -> x1, waiting for transfers between devices: none -> 33.5 us  [per_device(): lax.all_gather(partial_panel[:panel_width], 'tok')]
    psum x1, waiting for transfers between devices: 102 us -> 94.8 us  [per_device(): remainder = lax.psum(partial_panel[panel_width:], 'tok') / total_count]
  transfers between devices with their start and end apart: 8 -> 9, of which waited for: 8 -> 9; matrix products, arithmetic and copies ran while one was open for 5% -> 6% of each run, Pallas kernels for 0% -> 0%
where the time goes in v1:
time: 525 us; the launch traced here: 524 us
  waiting for transfers between devices  382 us (73%)
  matrix products  86.5 us (16%)
  local copies, waits for them, and re-layouts  25.9 us (5%)
  between operations  14.8 us (3%)
  other arithmetic  14.2 us (3%)
    psum x1, waiting for transfers between devices, per_device(): remainder = lax.psum(partial_panel[panel_width:], 'tok') / total_count  94.8 us
    all_gather x3, waiting for transfers between devices, per_device(): lax.all_gather(iterate.astype(jnp.bfloat16), 'col', axis=0, tiled=True)  64.2 us
    all_gather x1, waiting for transfers between devices, per_device(): lax.all_gather(activations[:, :panel_width], 'col', axis=1, tiled=True)  51 us
    all_gather x1, waiting for transfers between devices, per_device(): diagonal_block = lax.all_gather(block_part, 'col', axis=0, tiled=True)  46.9 us
    all_gather x1, waiting for transfers between devices, per_device(): inverse = lax.all_gather(iterate, 'col', axis=0, tiled=True)  46.7 us
    all_gather x1, waiting for transfers between devices, per_device(): lax.all_gather(pruned, 'col', axis=1, tiled=True).astype(jnp.float32)  44.9 us
    all_gather x1, waiting for transfers between devices, per_device(): lax.all_gather(partial_panel[:panel_width], 'tok')  33.5 us
    dot_general x1, matrix products, per_device(): lax.dot_general(factor_rows, hessian_panel, (((1,), (1,)), ((), ())), pre...  30.5 us
  transfers between devices with their start and end apart: 9, of which 9 were waited for; matrix products, arithmetic and copies ran while one was open for 6% of the time, Pallas kernels for 0%

profile of v1, /device:TPU:0, one launch (start us, length us, event | category | flops | bytes accessed | tf_op | source)
XLA Modules:
  0.0 523.9 jit_solution(9050981671413676568)
XLA Ops:
  6.5 0.0 all-gather.12.cloned.1.call-start
  6.5 1.9 slice.17
  8.4 0.0 all-gather.12.cloned.1.call-update
  8.4 0.0 all-gather.24.cloned.1.call-start
  8.5 51.0 %all-gather.12.cloned.1.call-done = bf16[2048,1024]{1,0:T(8,128)(2,1)} async-done(((bf16[2048,128]{1,0:T(8,128)(2,1)}), bf16[2048,1024]{1,0:T(8,128)(2,1)}) %all-gather.12.cloned.1.call-update) | async-done | bytes 4194320 | tf_op jit(solution)/shard_map/all_gather | solution.py:19
  59.5 7.6 %fusion.31 = f32[1024,1024]{1,0:T(8,128)S(1)} fusion(bf16[2048,1024]{1,0:T(8,128)(2,1)} %param.3, bf16[2048,1024]{1,0:T(8,128)(2,1)} %all-gather.12.cloned.1.call-done), kind=kOutput, calls=%fused_computation.42 | convolution fusion | flops 4294967296 | bytes 12582912 | tf_op jit(solution)/shard_map/dot_general | solution.py:17
  67.1 0.0 copy-start
  67.1 2.0 copy-done
  69.1 0.8 slice.22
  69.9 0.0 all-gather.24.cloned.1.call-update
  70.0 0.0 all-gather.14.cloned.1.call-start
  70.0 33.5 %all-gather.24.cloned.1.call-done = f32[512,1024]{1,0:T(8,128)} async-done(((f32[128,1024]{1,0:T(8,128)}), f32[512,1024]{1,0:T(8,128)}) %all-gather.24.cloned.1.call-update) | async-done | bytes 2097168 | tf_op jit(solution)/shard_map/all_gather | solution.py:23
  103.5 1.8 reduce_sum.27
  105.3 0.8 broadcast_multiply_fusion.1
  106.1 0.0 all-gather.14.cloned.1.call-update
  106.1 0.0 all-gather.16.cloned.1.call-start
  106.2 46.9 %all-gather.14.cloned.1.call-done = f32[1024,1024]{1,0:T(8,128)} async-done(((f32[128,1024]{1,0:T(8,128)}), f32[1024,1024]{1,0:T(8,128)}) %all-gather.14.cloned.1.call-update) | async-done | bytes 4194320 | tf_op jit(solution)/shard_map/all_gather | solution.py:24
  153.2 16.8 %gather_fusion = f32[1024]{0:T(1024)S(1)} fusion(f32[1024,1024]{1,0:T(8,128)} %all-gather.14.cloned.1.call-done, s32[1024]{0:T(1024)S(1)} %bitcast.17), kind=kCustom, calls=%fused_computation | custom fusion | bytes 16384 | tf_op jit(solution)/shard_map/jit(diagonal)/cond/branch_0_fun/gather | solution.py:26
  170.0 0.7 reduce_sum.28
  171.4 4.0 multiply_reduce_fusion
  176.1 4.7 fusion.16
  180.8 2.5 fusion.28
  183.3 0.0 all-gather.16.cloned.1.call-update
  183.4 0.0 all-gather.18.cloned.1.call-start
  183.4 4.7 fusion.15
  188.1 23.4 %all-gather.16.cloned.1.call-done = bf16[1024,1024]{1,0:T(8,128)(2,1)} async-done(((bf16[128,1024]{1,0:T(8,128)(2,1)}), bf16[1024,1024]{1,0:T(8,128)(2,1)}) %all-gather.16.cloned.1.call-update) | async-done | bytes 2097168 | tf_op jit(solution)/shard_map/all_gather | solution.py:36
  211.5 3.3 fusion.29
  214.8 0.0 all-gather.18.cloned.1.call-update
  214.8 0.2 all-gather.20.cloned.1.call-start
  215.1 4.7 fusion.14
  219.8 23.8 %all-gather.18.cloned.1.call-done = bf16[1024,1024]{1,0:T(8,128)(2,1)} async-done(((bf16[128,1024]{1,0:T(8,128)(2,1)}), bf16[1024,1024]{1,0:T(8,128)(2,1)}) %all-gather.18.cloned.1.call-update) | async-done | bytes 2097168 | tf_op jit(solution)/shard_map/all_gather | solution.py:36
  243.6 3.3 fusion.30
  247.0 0.0 all-gather.20.cloned.1.call-update
  247.0 0.0 all-reduce.2.cloned.1.call-start
  247.0 4.4 slice.23
  251.4 0.0 all-reduce.2.cloned.1.call-update
  251.4 0.0 all-gather.10.cloned.1.call-start
  251.5 2.3 fusion.17
  253.8 0.0 all-gather.10.cloned.1.call-update
  253.8 0.0 all-gather.22.cloned.1.call-start
  253.9 4.9 fusion.13
  258.7 16.9 %all-gather.20.cloned.1.call-done = bf16[1024,1024]{1,0:T(8,128)(2,1)} async-done(((bf16[128,1024]{1,0:T(8,128)(2,1)}), bf16[1024,1024]{1,0:T(8,128)(2,1)}) %all-gather.20.cloned.1.call-update) | async-done | bytes 2097168 | tf_op jit(solution)/shard_map/all_gather | solution.py:36
  275.7 3.4 convolution_subtract_fusion
  279.1 0.0 all-gather.22.cloned.1.call-update
  279.1 94.8 %all-reduce.2.cloned.1.call-done = f32[896,1024]{1,0:T(8,128)} async-done(((f32[896,1024]{1,0:T(8,128)}), f32[896,1024]{1,0:T(8,128)}) %all-reduce.2.cloned.1.call-update) | async-done | bytes 3670032 | tf_op jit(solution)/shard_map/psum | solution.py:42
  373.9 4.6 broadcast_multiply_fusion
  378.5 0.0 copy-start.2
  378.5 44.9 %all-gather.10.cloned.1.call-done = bf16[2048,1024]{1,0:T(8,128)(2,1)} async-done(((bf16[2048,128]{1,0:T(8,128)(2,1)}), bf16[2048,1024]{1,0:T(8,128)(2,1)}) %all-gather.10.cloned.1.call-update) | async-done | bytes 4194320 | tf_op jit(solution)/shard_map/all_gather | solution.py:47
  423.3 46.7 %all-gather.22.cloned.1.call-done = f32[1024,1024]{1,0:T(8,128)} async-done(((f32[128,1024]{1,0:T(8,128)}), f32[1024,1024]{1,0:T(8,128)}) %all-gather.22.cloned.1.call-update) | async-done | bytes 4194320 | tf_op jit(solution)/shard_map/all_gather | solution.py:41
  470.0 0.0 copy-start.1
  470.0 0.0 copy-start.3
  470.0 16.8 %fusion.32 = f32[2048,1024]{1,0:T(8,128)S(1)} fusion(bf16[2048,1024]{1,0:T(8,128)(2,1)} %all-gather.10.cloned.1.call-done, f32[1024,1024]{1,0:T(8,128)} %all-gather.22.cloned.1.call-done), kind=kOutput, calls=%fused_computation.43 | convolution fusion | flops 25769803776 | bytes 16777216 | tf_op jit(solution)/shard_map/dot_general | solution.py:48
  486.8 0.0 copy-done.2
  486.8 0.0 copy-done.1
  486.8 0.0 copy-done.3
  486.9 30.5 %multiply_convert_fusion = bf16[2048,1024]{1,0:T(8,128)(2,1)} fusion(bf16[2048,1024]{1,0:T(8,128)(2,1)S(1)} %copy-done.3, s32[2048,1024]{1,0:T(8,128)} %param.5, f32[2048,1024]{1,0:T(8,128)S(1)} %fusion.32, f32[896,1024]{1,0:T(8,128)S(1)} %copy-done.1, f32[128,1024]{1,0:T(8,128)S(1)} %copy-done.2), kind=kOutput, calls=%fused_computation.1 | convolution fusion | flops 25781338112 | bytes 29360128 | tf_op jit(solution)/shard_map/dot_general | solution.py:49
  (2 shorter events, 0.0 us)
Async XLA Ops:
  6.5 53.0 %all-gather.12.cloned.1.call-start = ((), (), s32[]{:S(2)}) async-start(), calls=%async_computation.1 | async-start | bytes 4718592 | tf_op jit(solution)/shard_map/all_gather | solution.py:19
  8.4 95.0 %all-gather.24.cloned.1.call-start = ((), (), s32[]{:S(2)}) async-start(), calls=%async_computation.8 | async-start | bytes 2621440 | tf_op jit(solution)/shard_map/all_gather | solution.py:23
  67.1 2.0 copy-start
  70.0 83.2 %all-gather.14.cloned.1.call-start = ((), (), s32[]{:S(2)}) async-start(), calls=%async_computation.2 | async-start | bytes 4718592 | tf_op jit(solution)/shard_map/all_gather | solution.py:24
  106.1 105.3 %all-gather.16.cloned.1.call-start = ((), (), s32[]{:S(2)}) async-start(), calls=%async_computation.3 | async-start | bytes 2359296 | tf_op jit(solution)/shard_map/all_gather | solution.py:36
  183.4 60.3 %all-gather.18.cloned.1.call-start = ((), (), s32[]{:S(2)}) async-start(), calls=%async_computation.4 | async-start | bytes 2359296 | tf_op jit(solution)/shard_map/all_gather | solution.py:36
  214.8 60.8 %all-gather.20.cloned.1.call-start = ((), (), s32[]{:S(2)}) async-start(), calls=%async_computation.5 | async-start | bytes 2359296 | tf_op jit(solution)/shard_map/all_gather | solution.py:36
  247.0 126.9 %all-reduce.2.cloned.1.call-start = ((), (), s32[]{:S(2)}) async-start(), calls=%async_computation.7 | async-start | bytes 7340032 | tf_op jit(solution)/shard_map/psum | solution.py:42
  251.4 171.9 %all-gather.10.cloned.1.call-start = ((), (), s32[]{:S(2)}) async-start(), calls=%async_computation | async-start | bytes 4718592 | tf_op jit(solution)/shard_map/all_gather | solution.py:47
  253.8 216.2 %all-gather.22.cloned.1.call-start = ((), (), s32[]{:S(2)}) async-start(), calls=%async_computation.6 | async-start | bytes 4718592 | tf_op jit(solution)/shard_map/all_gather | solution.py:41
  378.5 108.3 %copy-start.2 = (f32[128,1024]{1,0:T(8,128)S(1)}, f32[128,1024]{1,0:T(8,128)}, u32[]{:S(2)}) copy-start(f32[128,1024]{1,0:T(8,128)} %broadcast_multiply_fusion.1) | copy-start | bytes 1572868
  470.0 16.8 %copy-start.1 = (f32[896,1024]{1,0:T(8,128)S(1)}, f32[896,1024]{1,0:T(8,128)}, u32[]{:S(2)}) copy-start(f32[896,1024]{1,0:T(8,128)} %broadcast_multiply_fusion) | copy-start | bytes 11010052
  470.0 16.8 %copy-start.3 = (bf16[2048,1024]{1,0:T(8,128)(2,1)S(1)}, bf16[2048,1024]{1,0:T(8,128)(2,1)}, u32[]{:S(2)}) copy-start(bf16[2048,1024]{1,0:T(8,128)(2,1)} %param.4) | copy-start | bytes 12582916
Sparse Core Ops, SparseCore 0:
  8.9 50.5 all-gather.11
  70.1 33.3 all-gather.23
  106.3 46.8 all-gather.13
  183.5 27.9 all-gather.15
  215.0 28.6 all-gather.17
  247.1 28.5 all-gather.19
  278.8 95.0 all-reduce.1
  375.5 47.8 all-gather.9
  424.9 45.0 all-gather.21
